TPU v7x, 256 devices: a whole 4x4x8 slice. The times are simulated.
256 devices in a mesh: gx: 4 (over x), gy: 8 (over z), gz: 8 (over y, core).
Axes of the slice: x: 4, y: 4, z: 8, core: 2. Of those that a mesh axis runs over, the one named last changes fastest.
Arguments:
- src_fields: float32 [8192, 1080], P(('gx', 'gy', 'gz')), may hold values from -6 to 6
- owner_peer: int32 [8192, 8, 1], P(('gx', 'gy', 'gz')), may hold values from 0 to 31; in each aligned block of 256 rows (0 to 255, 256 to 511, ..., all dimensions but the last counted through in order) at most 9 rows name the same one
- src_local: int32 [8192, 8], P(('gx', 'gy', 'gz')), may hold values from 0 to 31
- jac: float32 [8192, 4096], P(('gx', 'gy', 'gz')), may hold values from 0.25 to 4
Outputs:
- remapped: float32 [8192, 1080], P(('gx', 'gy', 'gz'))
- nodal_accel: float32 [8192, 648], P(('gx', 'gy', 'gz'))
Inputs may be any that keep to these rules, and one draw needn't show every extreme that they name: owner_peer[r, k, 0] is the index, within the 32 devices that share target r's gz index (gx-major), of the device owning intersection k's source element; among the 256 intersections of one device's targets at most 9 name the same device, and some device reaches 9 in every draw.
All inputs are finite; a program needn't handle non-finite values.
Results may differ from a plain program's by a relative error of at most 0.0002.
Values sent between devices are 32-bit elements; how exact they have to be, the bound alone decides.
A program may use at most 64 MiB of HBM per device.

v0:
```python
import math

import jax
import jax.numpy as jnp
import ml_dtypes
import numpy as np
from jax import lax
from jax.experimental import pallas as pl
from jax.experimental.pallas import tpu as pltpu
from jax.sharding import PartitionSpec as P

EX = 4
EY = 4
EZ = 2
FIELDS = 5
NB = 216
QP = 512
OVL = 8
ELEMS = 32
WIDTH = FIELDS * NB
NX = 4
NY = 8
NZ = 8
CAP = 9
SLOTS = NX * NY * CAP
MESH = pl.DeviceIdType.MESH
F32 = jnp.float32
BF16 = jnp.bfloat16


def bern_table(points):
    cols = [math.comb(5, i) * points**i * (1.0 - points) ** (5 - i) for i in range(6)]
    return np.stack(cols, -1)


def remap_tables():
    mids = (np.arange(8) + 0.5) / 16.0
    src_one = []
    tgt_one = []
    for bit in range(2):
        target_pts = bit * 0.5 + mids
        source_pts = target_pts + 0.5 - bit
        src_one.append(bern_table(source_pts).T)
        tgt_one.append(bern_table(target_pts) / 16.0)
    source_list = []
    project_list = []
    for intersection in range(8):
        bit_x, bit_y, bit_z = (intersection >> 2 & 1, intersection >> 1 & 1, intersection & 1)
        source_list.append(np.kron(src_one[bit_x], np.kron(src_one[bit_y], src_one[bit_z])))
        project_list.append(np.kron(tgt_one[bit_x], np.kron(tgt_one[bit_y], tgt_one[bit_z])))
    return np.stack(source_list), np.stack(project_list)


def lower_integral(first, second):
    if first < 0 or first > 4:
        return 0.0
    return math.comb(4, first) * math.comb(5, second) / (10.0 * math.comb(9, first + second))


def force_table():
    mass_one = np.zeros((6, 6))
    grad_one = np.zeros((6, 6))
    for left in range(6):
        for right in range(6):
            mass_one[left, right] = (
                math.comb(5, left) * math.comb(5, right) / (11.0 * math.comb(10, left + right))
            )
            grad_one[left, right] = 5.0 * (
                lower_integral(left - 1, right) - lower_integral(left, right)
            )
    grad_x = np.kron(grad_one, np.kron(mass_one, mass_one))
    grad_y = np.kron(mass_one, np.kron(grad_one, mass_one))
    grad_z = np.kron(mass_one, np.kron(mass_one, grad_one))
    padded = [np.pad(g.T * 8.0, ((0, 0), (0, 40))) for g in (grad_x, grad_y, grad_z)]
    return np.concatenate(padded, 1)


def two_parts(table):
    high = table.astype(ml_dtypes.bfloat16)
    low = (table - high.astype(np.float64)).astype(ml_dtypes.bfloat16)
    return high, low


def halves(x):
    high = x.astype(BF16)
    return high, (x - high.astype(F32)).astype(BF16)


def dot3(a_high, a_low, b_high, b_low):
    total = jnp.dot(a_high, b_high, preferred_element_type=F32)
    total += jnp.dot(a_low, b_high, preferred_element_type=F32)
    return total + jnp.dot(a_high, b_low, preferred_element_type=F32)


def roll_sub(v, by):
    return v if by % 8 == 0 else pltpu.roll(v, by % 8, len(v.shape) - 2)


def pack_face(dim, a, high):
    sub = lax.broadcasted_iota(jnp.int32, (4, 1, 8, 256), 2)
    if dim == 0:
        return a[:, 3 if high else 0][:, None]
    if dim == 1:
        first = 6 if high else 0
        out = roll_sub(a[:, :1], -first)
        for e in range(1, 4):
            out = jnp.where(sub // 2 == e, roll_sub(a[:, e : e + 1], 2 * e - first), out)
        return out
    first = 1 if high else 0
    pairs = [
        jnp.where(
            sub % 2 == 0,
            roll_sub(a[:, 2 * e : 2 * e + 1], -first),
            roll_sub(a[:, 2 * e + 1 : 2 * e + 2], 1 - first),
        )
        for e in range(2)
    ]
    return jnp.concatenate(pairs, 1)


def neighbour_rows(dim, a, got, up):
    sub = lax.broadcasted_iota(jnp.int32, (4, 4, 8, 256), 2)
    if dim == 0:
        return jnp.concatenate([a[:, 1:], got] if up else [got, a[:, :3]], 1)
    if dim == 1:
        local = roll_sub(a, -2 if up else 2)
        first = 6 if up else 0
        away = [roll_sub(got, first - 2 * e) for e in range(4)]
        far = sub // 2 == (3 if up else 0)
    else:
        local = roll_sub(a, -1 if up else 1)
        first = 1 if up else 0
        away = [roll_sub(got[:, e // 2 : e // 2 + 1], first - e % 2) for e in range(4)]
        far = sub % 2 == (1 if up else 0)
    return jnp.where(far, jnp.concatenate(away, 1), local)


def whole_kernel(
    src_hbm, owner_ref, local_ref, jac_hbm, sh_hbm, sl_hbm, ph_hbm, pl_hbm, fh_hbm, fl_hbm,
    remapped_ref, accel_ref,
    b0, b1, b2, b3, b4, b5, b6, b7, send, arr, req_v, rreq_v, pos_v, req_s, pos_s,
    jac_v, sh_v, sl_v, ph_v, pl_v, fh_v, fl_v, rows_v,
    s0, s1, s2, s3, s4, s5, r0, r1, r2, r3, r4, r5,
    ring_send, ring_recv, req_send, req_recv, row_send, row_recv, copy_sem, load_sem,
    face_send, face_recv,
):
    x = lax.axis_index("gx")
    z = lax.axis_index("gy")
    y = lax.axis_index("gz")
    right = lax.rem(z + 1, NY)
    left = lax.rem(z + NY - 1, NY)
    ahead = [lax.rem(x + i, NX) for i in range(NX)]
    blk = [b0, b1, b2, b3, b4, b5, b6, b7]
    sends = [s0, s1, s2, s3, s4, s5]
    recvs = [r0, r1, r2, r3, r4, r5]
    place = (x, z, y)
    counts = (NX, NY, NZ)
    names = ("gx", "gy", "gz")

    def there(dim, side):
        return place[dim] + 2 * side - 1

    def inside(dim, side):
        return place[dim] < counts[dim] - 1 if side else place[dim] > 0

    barrier = pltpu.get_barrier_semaphore()
    for axis, where in (("gy", left), ("gy", right), ("gx", ahead[1]), ("gx", ahead[2]), ("gx", ahead[3])):
        pl.semaphore_signal(barrier, inc=1, device_id={axis: where}, device_id_type=MESH)
    near = 5
    for side in range(2):

        @pl.when(inside(2, side))
        def _():
            pl.semaphore_signal(
                barrier, inc=1, device_id={"gz": there(2, side)}, device_id_type=MESH
            )

        near = near + jnp.where(inside(2, side), 1, 0)

    own_load = pltpu.make_async_copy(src_hbm, b0, load_sem.at[0])
    own_load.start()
    loads = [
        pltpu.make_async_copy(a, b, load_sem.at[1 + i])
        for i, (a, b) in enumerate(
            zip(
                (jac_hbm, sh_hbm, sl_hbm, ph_hbm, pl_hbm, fh_hbm, fl_hbm),
                (jac_v, sh_v, sl_v, ph_v, pl_v, fh_v, fl_v),
            )
        )
    ]

    count = ELEMS * OVL
    owner = jnp.concatenate([owner_ref[k] for k in range(OVL)], 1)
    wanted = jnp.concatenate([local_ref[k : k + 1, :] for k in range(OVL)], 1).astype(F32)
    group = ((owner // NY - x + NX) & 3) * NY + ((z - (owner & 7) + NY) & 7)
    hits = jnp.where(group == lax.broadcasted_iota(jnp.int32, (NX * NY, count), 0), 1.0, 0.0)
    tri = lax.broadcasted_iota(jnp.int32, (count, count), 0) < lax.broadcasted_iota(
        jnp.int32, (count, count), 1
    )
    earlier = jnp.dot(
        hits.astype(BF16), jnp.where(tri, 1.0, 0.0).astype(BF16), preferred_element_type=F32
    )
    rank = jnp.sum(earlier * hits, 0, keepdims=True).astype(jnp.int32)
    slot = lax.broadcasted_iota(jnp.int32, (128, count), 0)
    placed = jnp.where(slot == rank, wanted, 0.0)
    req_v[...] = lax.dot_general(
        hits.astype(BF16), placed.astype(BF16), (((1,), (1,)), ((), ())), preferred_element_type=F32
    ).astype(jnp.int32)
    pos_v[...] = group * CAP + jnp.minimum(rank, CAP - 1)

    pl.semaphore_wait(barrier, near)

    def ask(i):
        return pltpu.make_async_remote_copy(
            src_ref=req_v.at[pl.ds(8 * i, 8)],
            dst_ref=rreq_v.at[i - 1],
            send_sem=req_send.at[i - 1],
            recv_sem=req_recv.at[i - 1],
            device_id={"gx": ahead[i]},
            device_id_type=MESH,
        )

    for i in range(1, NX):
        ask(i).start()

    def hop(way, d, c):
        dst = (d + 1) % 8 if way == 0 else (d + 7) % 8
        rows = pl.ds(16 * c, 16)
        return pltpu.make_async_remote_copy(
            src_ref=blk[d].at[rows],
            dst_ref=blk[dst].at[rows],
            send_sem=ring_send.at[way, d, c],
            recv_sem=ring_recv.at[way, dst, c],
            device_id={"gy": right if way == 0 else left},
            device_id_type=MESH,
        )

    hops = []

    def go(way, d, c):
        one = hop(way, d, c)
        one.start()
        hops.append(one)

    def arrived(way, d, c):
        hop(way, (d + 7) % 8 if way == 0 else (d + 1) % 8, c).wait_recv()

    own_load.wait()
    for c in range(2):
        go(0, 0, c)
        go(1, 0, c)
    mine_first = pltpu.make_async_copy(req_v.at[pl.ds(0, 8)], req_s.at[0], copy_sem.at[0])
    mine_first.start()
    pos_copy = pltpu.make_async_copy(pos_v, pos_s, copy_sem.at[4])
    pos_copy.start()
    for one in loads:
        one.start()
    for dim in range(3):
        for side in range(2):

            @pl.when(jnp.logical_not(inside(dim, side)))
            def _():
                recvs[2 * dim + side][...] = jnp.zeros_like(recvs[2 * dim + side])

    mine_first.wait()
    pos_copy.wait()
    for i in range(1, NX):
        ask(i).wait_recv()
        one = pltpu.make_async_copy(rreq_v.at[i - 1], req_s.at[i], copy_sem.at[i])
        one.start()
        one.wait()

    def reply(i, d):
        return pltpu.make_async_remote_copy(
            src_ref=send.at[pl.ds(((i - 1) * 8 + d) * CAP, CAP)],
            dst_ref=arr.at[pl.ds((i * 8 + d) * CAP, CAP)],
            send_sem=row_send.at[i - 1, d],
            recv_sem=row_recv.at[i - 1, d],
            device_id={"gx": ahead[NX - i]},
            device_id_type=MESH,
        )

    def answer(d):
        def one_slot(s, carry):
            for i in range(NX):
                row = blk[d][pl.ds(req_s[i, d, s] & (ELEMS - 1), 1), :]
                if i == 0:
                    arr[d * CAP + s] = row
                else:
                    send[((i - 1) * 8 + d) * CAP + s] = row
            return carry

        lax.fori_loop(0, CAP, one_slot, 0)
        for i in (2, 1, 3):
            reply(i, d).start()

    answer(0)
    for j in range(1, 4):
        for c in range(2):
            arrived(0, j, c)
            if j < 3 or c == 0:
                go(0, j, c)
            arrived(1, 8 - j, c)
            if j < 3 or c == 1:
                go(1, 8 - j, c)
        answer(j)
        answer(8 - j)
    arrived(0, 4, 0)
    arrived(1, 4, 1)
    answer(4)

    for one in loads:
        one.wait()
    for i in range(1, NX):
        for d in range(8):
            reply(i, d).wait_recv()

    total = jnp.zeros(((FIELDS + 1) * ELEMS, NB), F32)
    for k in range(OVL):
        buf = rows_v.at[k % 2]
        for r in range(ELEMS):
            buf[pl.ds(r, 1), :] = arr[jnp.clip(pos_s[0, k * ELEMS + r], 0, SLOTS - 1)]
        rows = buf[...]
        lhs = jnp.concatenate([rows[:, f * NB : (f + 1) * NB] for f in range(FIELDS)], 0)
        values = dot3(*halves(lhs), sh_v[k], sl_v[k])
        weight = jac_v[:, k * QP : (k + 1) * QP]
        scaled = [values[f * ELEMS : (f + 1) * ELEMS] * weight for f in range(FIELDS)]
        total += dot3(*halves(jnp.concatenate(scaled + [weight], 0)), ph_v[k], pl_v[k])
    lumped = total[FIELDS * ELEMS :]
    fields = [total[f * ELEMS : (f + 1) * ELEMS] / lumped for f in range(FIELDS)]
    remapped_ref[...] = jnp.concatenate(fields, 1)
    force = dot3(*halves(fields[0] * fields[1]), fh_v[...], fl_v[...])
    mass = jnp.concatenate([lumped, jnp.zeros((ELEMS, 40), F32)], 1)
    a = jnp.stack([force[:, :256], force[:, 256:512], force[:, 512:], mass], 0)
    a = a.reshape(4, 4, 8, 256)

    lane = lax.broadcasted_iota(jnp.int32, (4, 4, 8, 256), 3)
    lane_in = (lane // 36, (lane // 6) % 6, lane % 6)

    def face(dim, side):
        n = 2 * dim + side
        return pltpu.make_async_remote_copy(
            src_ref=sends[n],
            dst_ref=recvs[2 * dim + 1 - side],
            send_sem=face_send.at[n],
            recv_sem=face_recv.at[2 * dim + 1 - side],
            device_id={names[dim]: jnp.clip(there(dim, side), 0, counts[dim] - 1)},
            device_id_type=MESH,
        )

    for dim in range(3):
        for side in range(2):
            sends[2 * dim + side][...] = pack_face(dim, a, side == 1)

            @pl.when(inside(dim, side))
            def _():
                face(dim, side).start()

        for side in range(2):

            @pl.when(inside(dim, side))
            def _():
                face(dim, 1 - side).wait_recv()

        by = (180, 30, 5)[dim]
        up = neighbour_rows(dim, a, recvs[2 * dim + 1][...], True)
        down = neighbour_rows(dim, a, recvs[2 * dim][...], False)
        gain = jnp.where(lane_in[dim] == 5, pltpu.roll(up, by, 3), 0.0)
        gain += jnp.where(lane_in[dim] == 0, pltpu.roll(down, 256 - by, 3), 0.0)
        a = a + gain

    mass = a[3].reshape(ELEMS, 256)[:, :NB]
    accel = [a[c].reshape(ELEMS, 256)[:, :NB] / mass for c in range(3)]
    accel_ref[...] = jnp.concatenate(accel, 1)

    for dim in range(3):
        for side in range(2):

            @pl.when(inside(dim, side))
            def _():
                face(dim, side).wait_send()

    for one in hops:
        one.wait_send()
    for i in range(1, NX):
        ask(i).wait_send()
        for d in range(8):
            reply(i, d).wait_send()


def per_device(src_fields, owner_peer, src_local, jac):
    source_tab, project_tab = remap_tables()
    tables = [*two_parts(source_tab), *two_parts(project_tab), *two_parts(force_table())]
    vmem = pl.BlockSpec(memory_space=pltpu.VMEM)
    hbm = pl.BlockSpec(memory_space=pltpu.HBM)
    dma = pltpu.SemaphoreType.DMA
    tiles = [1, 1, 1, 1, 2, 2]
    return pl.pallas_call(
        whole_kernel,
        out_shape=(
            jax.ShapeDtypeStruct((ELEMS, WIDTH), F32),
            jax.ShapeDtypeStruct((ELEMS, 3 * NB), F32),
        ),
        in_specs=[hbm, vmem, vmem] + [hbm] * 7,
        out_specs=(vmem, vmem),
        scratch_shapes=[pltpu.VMEM((ELEMS, WIDTH), F32) for _ in range(8)]
        + [
            pltpu.VMEM(((NX - 1) * NY * CAP, 1, WIDTH), F32),
            pltpu.VMEM((SLOTS, 1, WIDTH), F32),
            pltpu.VMEM((NX * NY, 128), jnp.int32),
            pltpu.VMEM((NX - 1, NY, 128), jnp.int32),
            pltpu.VMEM((1, OVL * ELEMS), jnp.int32),
            pltpu.SMEM((NX, NY, 128), jnp.int32),
            pltpu.SMEM((1, OVL * ELEMS), jnp.int32),
            pltpu.VMEM((ELEMS, OVL * QP), F32),
            pltpu.VMEM((OVL, NB, QP), BF16),
            pltpu.VMEM((OVL, NB, QP), BF16),
            pltpu.VMEM((OVL, QP, NB), BF16),
            pltpu.VMEM((OVL, QP, NB), BF16),
            pltpu.VMEM((NB, 768), BF16),
            pltpu.VMEM((NB, 768), BF16),
            pltpu.VMEM((2, ELEMS, WIDTH), F32),
        ]
        + [pltpu.VMEM((4, t, 8, 256), F32) for t in tiles + tiles]
        + [
            dma((2, 8, 2)),
            dma((2, 8, 2)),
            dma((NX - 1,)),
            dma((NX - 1,)),
            dma((NX - 1, NY)),
            dma((NX - 1, NY)),
            dma((5,)),
            dma((8,)),
            dma((6,)),
            dma((6,)),
        ],
        compiler_params=pltpu.CompilerParams(
            collective_id=0, has_side_effects=True, vmem_limit_bytes=58 << 20
        ),
        name="whole",
    )(
        src_fields,
        jnp.transpose(owner_peer, (1, 2, 0)),
        jnp.transpose(src_local, (1, 0)),
        jac,
        *[jnp.asarray(t) for t in tables],
    )


def solution(mesh):
    placed = (
        P(("gx", "gy", "gz"), None),
        P(("gx", "gy", "gz"), None, None),
        P(("gx", "gy", "gz"), None),
        P(("gx", "gy", "gz"), None),
    )
    return jax.shard_map(
        per_device,
        mesh=mesh,
        in_specs=placed,
        out_specs=(P(("gx", "gy", "gz"), None), P(("gx", "gy", "gz"), None)),
        check_vma=False,
    )
```

profile of v0, /device:TPU:1, one launch (start us, length us, event | category | flops | bytes accessed | tf_op | source)
XLA Modules:
  0.0 50.2 jit_solution(14082848573300122324)
XLA Ops:
  0.6 46.5 %whole.1 = (f32[32,1080]{1,0:T(8,128)}, f32[32,648]{1,0:T(8,128)}) custom-call(f32[32,1080]{1,0:T(8,128)} %src_hbm.1, s32[8,1,32]{2,1,0:T(1,128)} %bitcast.2, s32[8,32]{1,0:T(8,128)} %bitcast.3, f32[32,4096]{1,0:T(8,128)} %jac_hbm.1, bf16[8,216,512]{2,1,0:T(8,128)(2,1)} %constant.12.clone.sh_hbm, bf16[8,216,512]{2,1,0:T(8,128)(2,1)} %constant.13.clone.sl_hbm, ...), custom_call_target="tpu_custom_call" | custom-call | tf_op jit(solution)/shard_map/whole/pallas_call | solution.py:398
  47.1 1.6 %copy.14 = f32[32,1080]{1,0:T(8,128)} copy(f32[32,1080]{1,0:T(8,128)} %get-tuple-element.4) | data formatting | bytes 276480
  48.7 1.5 %copy.15 = f32[32,648]{1,0:T(8,128)} copy(f32[32,648]{1,0:T(8,128)} %get-tuple-element.5) | data formatting | bytes 165888
where the time goes:
time: 50.4 us; the launch traced here: 50.2 us
  Pallas kernels  46.5 us (92%)
  local copies, waits for them, and re-layouts  3.12 us (6%)
  between operations  0.64 us (1%)
    pallas_call x1, Pallas kernels, per_device(): pl.pallas_call(whole_kernel, out_shape=(jax.ShapeDtypeStruct((ELEMS, WIDT...  46.5 us
    unnamed x2, local copies, waits for them, and re-layouts  3.12 us

commit v1 on v0

v1 whole, which is shorter than its diff:
```python
import math

import jax
import jax.numpy as jnp
import ml_dtypes
import numpy as np
from jax import lax
from jax.experimental import pallas as pl
from jax.experimental.pallas import tpu as pltpu
from jax.sharding import PartitionSpec as P

EX = 4
EY = 4
EZ = 2
FIELDS = 5
NB = 216
QP = 512
OVL = 8
ELEMS = 32
WIDTH = FIELDS * NB
WA = 512
WB = 640
TAIL = WA - 2 * NB
NX = 4
NY = 8
NZ = 8
CAP = 9
SLOTS = NX * NY * CAP
MESH = pl.DeviceIdType.MESH
OFFSETS = [
    (i, j, k) for i in (-1, 1, 0) for j in (-1, 1, 0) for k in (-1, 1, 0) if (i, j, k) != (0, 0, 0)
]
F32 = jnp.float32
BF16 = jnp.bfloat16


def bern_table(points):
    cols = [math.comb(5, i) * points**i * (1.0 - points) ** (5 - i) for i in range(6)]
    return np.stack(cols, -1)


def remap_tables():
    mids = (np.arange(8) + 0.5) / 16.0
    src_one = []
    tgt_one = []
    for bit in range(2):
        target_pts = bit * 0.5 + mids
        source_pts = target_pts + 0.5 - bit
        src_one.append(bern_table(source_pts).T)
        tgt_one.append(bern_table(target_pts) / 16.0)
    source_list = []
    project_list = []
    for intersection in range(8):
        bit_x, bit_y, bit_z = (intersection >> 2 & 1, intersection >> 1 & 1, intersection & 1)
        source_list.append(np.kron(src_one[bit_x], np.kron(src_one[bit_y], src_one[bit_z])))
        project_list.append(np.kron(tgt_one[bit_x], np.kron(tgt_one[bit_y], tgt_one[bit_z])))
    return np.stack(source_list), np.stack(project_list)


def lower_integral(first, second):
    if first < 0 or first > 4:
        return 0.0
    return math.comb(4, first) * math.comb(5, second) / (10.0 * math.comb(9, first + second))


def force_table():
    mass_one = np.zeros((6, 6))
    grad_one = np.zeros((6, 6))
    for left in range(6):
        for right in range(6):
            mass_one[left, right] = (
                math.comb(5, left) * math.comb(5, right) / (11.0 * math.comb(10, left + right))
            )
            grad_one[left, right] = 5.0 * (
                lower_integral(left - 1, right) - lower_integral(left, right)
            )
    grad_x = np.kron(grad_one, np.kron(mass_one, mass_one))
    grad_y = np.kron(mass_one, np.kron(grad_one, mass_one))
    grad_z = np.kron(mass_one, np.kron(mass_one, grad_one))
    padded = [np.pad(g.T * 8.0, ((0, 0), (0, 40))) for g in (grad_x, grad_y, grad_z)]
    return np.concatenate(padded, 1)


def two_parts(table):
    high = table.astype(ml_dtypes.bfloat16)
    low = (table - high.astype(np.float64)).astype(ml_dtypes.bfloat16)
    return high, low


def dot3(x, b_high, b_low):
    high = x.astype(BF16)
    low = (x - high.astype(F32)).astype(BF16)
    rows = x.shape[0]
    first = jnp.dot(jnp.concatenate([high, low], 0), b_high, preferred_element_type=F32)
    return first[:rows] + first[rows:] + jnp.dot(high, b_low, preferred_element_type=F32)


def roll_sub(v, by):
    return v if by % 8 == 0 else pltpu.roll(v, by % 8, len(v.shape) - 2)


def roll_lane(v, by):
    return v if by % 256 == 0 else pltpu.roll(v, by % 256, len(v.shape) - 1)


def shared_inside(dim, a):
    lane = lax.broadcasted_iota(jnp.int32, a.shape, 3)
    sub = lax.broadcasted_iota(jnp.int32, a.shape, 2)
    if dim == 0:
        edge = jnp.zeros_like(a[:, :1])
        up, down = jnp.concatenate([a[:, 1:], edge], 1), jnp.concatenate([edge, a[:, :3]], 1)
    elif dim == 1:
        up = jnp.where(sub // 2 == 3, 0.0, roll_sub(a, -2))
        down = jnp.where(sub // 2 == 0, 0.0, roll_sub(a, 2))
    else:
        up = jnp.where(sub % 2 == 1, 0.0, roll_sub(a, -1))
        down = jnp.where(sub % 2 == 0, 0.0, roll_sub(a, 1))
    step = (36, 6, 1)[dim]
    at = (lane // step) % 6
    gain = jnp.where(at == 5, roll_lane(up, 5 * step), 0.0)
    return a + gain + jnp.where(at == 0, roll_lane(down, -5 * step), 0.0)


def pack_x(a, side):
    lane = lax.broadcasted_iota(jnp.int32, (8, 256), 1)
    out = jnp.zeros((8, 256), F32)
    for c in range(4):
        out = jnp.where(lane // 36 == c, roll_lane(a[c, 3 * side], 36 * (c - 5 * side)), out)
    return out


def pack_y(a, side):
    lane = lax.broadcasted_iota(jnp.int32, (8, 256), 1)
    sub = lax.broadcasted_iota(jnp.int32, (8, 256), 0)
    out = jnp.zeros((8, 256), F32)
    for c in range(4):
        rows = roll_sub(a[c, 0], -6 * side)
        for e in range(1, 4):
            rows = jnp.where(sub // 2 == e, roll_sub(a[c, e], 2 * e - 6 * side), rows)
        out = jnp.where((lane // 6) % 6 == c, roll_lane(rows, 6 * (c - 5 * side)), out)
    return out


def pack_z(a, side):
    lane = lax.broadcasted_iota(jnp.int32, (8, 256), 1)
    sub = lax.broadcasted_iota(jnp.int32, (8, 256), 0)
    halves_z = []
    for h in range(2):
        out = jnp.zeros((8, 256), F32)
        for c in range(4):
            even, odd = a[c, 2 * h], a[c, 2 * h + 1]
            rows = jnp.where(sub % 2 == 0, roll_sub(even, -side), roll_sub(odd, 1 - side))
            out = jnp.where(lane % 6 == c, roll_lane(rows, c - 5 * side), out)
        halves_z.append(out)
    return jnp.stack(halves_z, 0)


def turned(tile, sy, sz):
    lane = lax.broadcasted_iota(jnp.int32, (8, 256), 1)
    sub = lax.broadcasted_iota(jnp.int32, (8, 256), 0)
    here = None
    rows = lanes = 0
    if sy is not None:
        here = (sub // 2 == 3 * sy) & ((lane // 6) % 6 == 5 * sy)
        rows, lanes = 12 * sy - 6, 60 * sy - 30
    if sz is not None:
        also = (sub % 2 == sz) & (lane % 6 == 5 * sz)
        here = also if here is None else here & also
        rows, lanes = rows + 2 * sz - 1, lanes + 10 * sz - 5
    return jnp.where(here, roll_lane(roll_sub(tile, rows), lanes), 0.0)


def unpack_x(got, side):
    lane = lax.broadcasted_iota(jnp.int32, (8, 256), 1)
    face = lane // 36 == 5 * side
    parts = [jnp.where(face, roll_lane(got, 36 * (5 * side - c)), 0.0) for c in range(4)]
    return jnp.stack(parts, 0)


def unpack_y(got, side):
    lane = lax.broadcasted_iota(jnp.int32, (8, 256), 1)
    sub = lax.broadcasted_iota(jnp.int32, (8, 256), 0)
    face = (lane // 6) % 6 == 5 * side
    comps = []
    for c in range(4):
        rows = jnp.where(face, roll_lane(got, 6 * (5 * side - c)), 0.0)
        tiles = [
            jnp.where(sub // 2 == 3 * side, roll_sub(rows, 6 * side - 2 * e), 0.0) for e in range(4)
        ]
        comps.append(jnp.stack(tiles, 0))
    return jnp.stack(comps, 0)


def unpack_z(got, side):
    lane = lax.broadcasted_iota(jnp.int32, (8, 256), 1)
    sub = lax.broadcasted_iota(jnp.int32, (8, 256), 0)
    face = lane % 6 == 5 * side
    comps = []
    for c in range(4):
        tiles = []
        for e in range(4):
            rows = jnp.where(face, roll_lane(got[e // 2], 5 * side - c), 0.0)
            tiles.append(jnp.where(sub % 2 == side, roll_sub(rows, side - e % 2), 0.0))
        comps.append(jnp.stack(tiles, 0))
    return jnp.stack(comps, 0)


def whole_kernel(
    src_hbm, owner_hbm, local_hbm, jac_hbm, sh_hbm, sl_hbm, ph_hbm, pl_hbm, fh_hbm, fl_hbm,
    remapped_ref, accel_ref,
    src_v, a0, a1, a2, a3, a4, a5, a6, a7, b0, b1, b2, b3, b4, b5, b6, b7, send_a, send_b, arr_a, arr_b, rows_a, rows_b, rows_c,
    req_v, rreq_v, pos_v, req_s, pos_s,
    owner_v, local_v, jac_v, sh_v, sl_v, ph_v, pl_v, fh_v, fl_v,
    face_x, face_y, face_z, got_x, got_y, got_z, got_xy, got_xz, got_yz, got_xyz,
    ring_send, ring_recv, req_send, req_recv, row_send, row_recv, copy_sem, load_sem,
    face_send, face_recv,
):
    x = lax.axis_index("gx")
    z = lax.axis_index("gy")
    y = lax.axis_index("gz")
    right = lax.rem(z + 1, NY)
    left = lax.rem(z + NY - 1, NY)
    ahead = [lax.rem(x + i, NX) for i in range(NX)]
    place = (x, z, y)
    counts = (NX, NY, NZ)
    names = ("gx", "gy", "gz")
    blk_a = [a0, a1, a2, a3, a4, a5, a6, a7]
    blk_b = [b0, b1, b2, b3, b4, b5, b6, b7]
    blocks = (blk_a, blk_b)
    outgoing = (send_a, send_b)
    incoming = (arr_a, arr_b)

    def has(offset):
        ok = None
        for here, count, o in zip(place, counts, offset):
            if o:
                one = here < count - 1 if o > 0 else here > 0
                ok = one if ok is None else ok & one
        return ok

    def at(offset):
        return {
            name: jnp.clip(here + o, 0, count - 1)
            for name, here, count, o in zip(names, place, counts, offset)
            if o
        }

    small = [
        pltpu.make_async_copy(owner_hbm, owner_v, load_sem.at[8]),
        pltpu.make_async_copy(local_hbm, local_v, load_sem.at[9]),
    ]
    for one in small:
        one.start()
    own_load = pltpu.make_async_copy(src_hbm, src_v, load_sem.at[0])
    own_load.start()

    for ref in (got_x, got_y, got_z, got_xy, got_xz, got_yz, got_xyz):
        ref[...] = jnp.zeros_like(ref)

    barrier = pltpu.get_barrier_semaphore()
    for axis, where in (
        ("gy", left), ("gy", right), ("gx", ahead[1]), ("gx", ahead[2]), ("gx", ahead[3])
    ):
        pl.semaphore_signal(barrier, inc=1, device_id={axis: where}, device_id_type=MESH)
    near = 5
    for offset in OFFSETS:
        if offset[2] or (offset[0] and offset[1]):

            @pl.when(has(offset))
            def _():
                pl.semaphore_signal(barrier, inc=1, device_id=at(offset), device_id_type=MESH)

            near = near + jnp.where(has(offset), 1, 0)

    count = ELEMS * OVL
    for one in small:
        one.wait()
    owner = jnp.concatenate([owner_v[k] for k in range(OVL)], 1)
    wanted = jnp.concatenate([local_v[k : k + 1, :] for k in range(OVL)], 1).astype(F32)
    group = ((owner // NY - x + NX) & 3) * NY + ((z - (owner & 7) + NY) & 7)
    hits = jnp.where(group == lax.broadcasted_iota(jnp.int32, (NX * NY, count), 0), 1.0, 0.0)
    tri = lax.broadcasted_iota(jnp.int32, (count, count), 0) < lax.broadcasted_iota(
        jnp.int32, (count, count), 1
    )
    earlier = jnp.dot(
        hits.astype(BF16), jnp.where(tri, 1.0, 0.0).astype(BF16), preferred_element_type=F32
    )
    rank = jnp.sum(earlier * hits, 0, keepdims=True).astype(jnp.int32)
    slot = lax.broadcasted_iota(jnp.int32, (128, count), 0)
    placed = jnp.where(slot == rank, wanted, 0.0)
    req_v[...] = lax.dot_general(
        hits.astype(BF16), placed.astype(BF16), (((1,), (1,)), ((), ())), preferred_element_type=F32
    ).astype(jnp.int32)
    pos_v[...] = group * CAP + jnp.minimum(rank, CAP - 1)

    own_load.wait()
    a0[...] = src_v[:, :WA]
    b0[...] = jnp.concatenate([src_v[:, WA:], jnp.zeros((ELEMS, WA + WB - WIDTH), F32)], 1)

    pl.semaphore_wait(barrier, near)

    def ask(i):
        return pltpu.make_async_remote_copy(
            src_ref=req_v.at[pl.ds(8 * i, 8)],
            dst_ref=rreq_v.at[i - 1],
            send_sem=req_send.at[i - 1],
            recv_sem=req_recv.at[i - 1],
            device_id={"gx": ahead[i]},
            device_id_type=MESH,
        )

    for i in range(1, NX):
        ask(i).start()

    def hop(part, way, d):
        dst = (d + 1) % 8 if way == 0 else (d + 7) % 8
        rows = pl.ds(16 * way, 16) if dst == 4 else pl.ds(0, ELEMS)
        return pltpu.make_async_remote_copy(
            src_ref=blocks[part][d].at[rows],
            dst_ref=blocks[part][dst].at[rows],
            send_sem=ring_send.at[part, way, d],
            recv_sem=ring_recv.at[part, way, dst],
            device_id={"gy": right if way == 0 else left},
            device_id_type=MESH,
        )

    hops = []

    def go(part, way, d):
        one = hop(part, way, d)
        one.start()
        hops.append(one)

    def pass_on(part, j):
        for way, d in ((0, j), (1, 8 - j)):
            hop(part, way, (d + 7) % 8 if way == 0 else (d + 1) % 8).wait_recv()
            if j < 4:
                go(part, way, d)

    go(0, 0, 0)
    go(0, 1, 0)
    asked = [
        pltpu.make_async_copy(rreq_v.at[i - 1], req_s.at[i], copy_sem.at[i]) for i in range(1, NX)
    ]
    mine_first = pltpu.make_async_copy(req_v.at[pl.ds(0, 8)], req_s.at[0], copy_sem.at[0])
    mine_first.start()
    pos_copy = pltpu.make_async_copy(pos_v, pos_s, copy_sem.at[4])
    pos_copy.start()
    loads = [
        pltpu.make_async_copy(a, b, load_sem.at[1 + i])
        for i, (a, b) in enumerate(
            zip(
                (jac_hbm, sh_hbm, sl_hbm, ph_hbm, pl_hbm, fh_hbm, fl_hbm),
                (jac_v, sh_v, sl_v, ph_v, pl_v, fh_v, fl_v),
            )
        )
    ]
    for one in loads:
        one.start()
    mine_first.wait()
    pos_copy.wait()
    for i in range(1, NX):
        ask(i).wait_recv()
        asked[i - 1].start()
    go(1, 0, 0)
    go(1, 1, 0)
    for one in asked:
        one.wait()

    def reply(part, i, d):
        return pltpu.make_async_remote_copy(
            src_ref=outgoing[part].at[pl.ds(((i - 1) * 8 + d) * CAP, CAP)],
            dst_ref=incoming[part].at[pl.ds((i * 8 + d) * CAP, CAP)],
            send_sem=row_send.at[part, i - 1, d],
            recv_sem=row_recv.at[part, i - 1, d],
            device_id={"gx": ahead[NX - i]},
            device_id_type=MESH,
        )

    def answer(part, d):
        block = blocks[part][d]

        def one_slot(s, carry):
            for i in range(NX):
                row = block[pl.ds(req_s[i, d, s] & (ELEMS - 1), 1), :]
                if i == 0:
                    incoming[part][d * CAP + s] = row
                else:
                    outgoing[part][((i - 1) * 8 + d) * CAP + s] = row
            return carry

        lax.fori_loop(0, CAP, one_slot, 0)
        for i in (2, 1, 3):
            reply(part, i, d).start()

    def settle(part):
        for i in range(1, NX):
            for d in range(8):
                reply(part, i, d).wait_recv()

    answer(0, 0)
    for j in range(1, 5):
        pass_on(0, j)
        answer(0, j)
        if j < 4:
            answer(0, 8 - j)
        pass_on(1, j)
        for d in ((0,), (1, 7), (2, 6), (3, 5, 4))[j - 1]:
            answer(1, d)

    for one in loads:
        one.wait()

    def remap(part, extra):
        fields = (2, 3)[part]
        held = (rows_a, rows_b)[part]
        total = jnp.zeros(((fields + extra) * ELEMS, NB), F32)
        for k in range(OVL):
            buf = held.at[k % 2]
            for r in range(ELEMS):
                at = jnp.clip(pos_s[0, k * ELEMS + r], 0, SLOTS - 1)
                buf[pl.ds(r, 1), :] = incoming[part][at]
                if part == 1:
                    rows_c[k % 2, pl.ds(r, 1), :] = arr_a[at, :, WA - 128 :]
            rows = buf[...]
            if part == 1:
                rows = jnp.concatenate([rows_c[k % 2][:, 128 - TAIL :], rows[:, : 3 * NB - TAIL]], 1)
            lhs = jnp.concatenate([rows[:, f * NB : (f + 1) * NB] for f in range(fields)], 0)
            values = dot3(lhs, sh_v[k], sl_v[k])
            weight = jac_v[:, k * QP : (k + 1) * QP]
            scaled = [values[f * ELEMS : (f + 1) * ELEMS] * weight for f in range(fields)]
            total += dot3(jnp.concatenate(scaled + [weight] * extra, 0), ph_v[k], pl_v[k])
        return [total[f * ELEMS : (f + 1) * ELEMS] for f in range(fields + extra)]

    settle(0)
    first, second, lumped = remap(0, 1)
    first = first / lumped
    second = second / lumped
    force = dot3(first * second, fh_v[...], fl_v[...])
    mass = jnp.concatenate([lumped, jnp.zeros((ELEMS, 40), F32)], 1)
    a = jnp.stack([force[:, :256], force[:, 256:512], force[:, 512:], mass], 0)
    a = a.reshape(4, 4, 8, 256)

    for dim in range(3):
        a = shared_inside(dim, a)

    def face(n):
        offset = OFFSETS[n]
        sx, sy, sz = ((o + 1) // 2 for o in offset)
        if offset[0]:
            src = face_x.at[sx]
            if not offset[1] and not offset[2]:
                dst = got_x.at[1 - sx]
            elif not offset[1]:
                dst = got_xz.at[1 - sx, 1 - sz]
            elif not offset[2]:
                dst = got_xy.at[1 - sx, 1 - sy]
            else:
                dst = got_xyz.at[1 - sx, 1 - sy, 1 - sz]
        elif offset[1]:
            src = face_y.at[sy]
            dst = got_yz.at[1 - sy, 1 - sz] if offset[2] else got_y.at[1 - sy]
        else:
            src, dst = face_z.at[sz], got_z.at[1 - sz]
        return pltpu.make_async_remote_copy(
            src_ref=src,
            dst_ref=dst,
            send_sem=face_send.at[n],
            recv_sem=face_recv.at[n],
            device_id=at(offset),
            device_id_type=MESH,
        )

    def start_faces(which):
        for n in which:

            @pl.when(has(OFFSETS[n]))
            def _():
                face(n).start()

    for side in range(2):
        face_x[side] = pack_x(a, side)
    start_faces([n for n, o in enumerate(OFFSETS) if o[0]])
    for side in range(2):
        face_y[side] = pack_y(a, side)
    start_faces([n for n, o in enumerate(OFFSETS) if not o[0] and o[1]])
    for side in range(2):
        face_z[side] = pack_z(a, side)
    start_faces([n for n, o in enumerate(OFFSETS) if not o[0] and not o[1]])
    for n, offset in enumerate(OFFSETS):

        @pl.when(has(offset))
        def _():
            face(n).wait_send()

    for one in hops:
        one.wait_send()
    for i in range(1, NX):
        ask(i).wait_send()
        for d in range(8):
            reply(0, i, d).wait_send()

    settle(1)
    rest = [one / lumped for one in remap(1, 0)]
    remapped_ref[...] = jnp.concatenate([first, second] + rest, 1)

    for n, offset in enumerate(OFFSETS):

        @pl.when(has([-o for o in offset]))
        def _():
            face(n).wait_recv()

    gain_x = []
    gain_y = []
    for side in range(2):
        got = got_x[side]
        for one in range(2):
            got = got + turned(got_xy[side, one], one, None) + turned(got_xz[side, one], None, one)
            got = got + turned(got_xyz[side, 0, one], 0, one) + turned(got_xyz[side, 1, one], 1, one)
        gain_x.append(unpack_x(got, side))
        got = got_y[side]
        for one in range(2):
            got = got + turned(got_yz[side, one], None, one)
        gain_y.append(unpack_y(got, side))
    none = jnp.zeros_like(gain_x[0])
    a = a + jnp.stack([gain_x[0], none, none, gain_x[1]], 1) + gain_y[0] + gain_y[1]
    a = a + unpack_z(got_z[0], 0) + unpack_z(got_z[1], 1)
    mass = a[3].reshape(ELEMS, 256)[:, :NB]
    accel = [a[c].reshape(ELEMS, 256)[:, :NB] / mass for c in range(3)]
    accel_ref[...] = jnp.concatenate(accel, 1)

    for i in range(1, NX):
        for d in range(8):
            reply(1, i, d).wait_send()


def store_kernel(remapped_ref, accel_ref, remapped_hbm, accel_hbm, sem):
    copies = [
        pltpu.make_async_copy(remapped_ref, remapped_hbm, sem.at[0]),
        pltpu.make_async_copy(accel_ref, accel_hbm, sem.at[1]),
    ]
    for one in copies:
        one.start()
    for one in copies:
        one.wait()


def store(remapped, accel):
    vmem = pl.BlockSpec(memory_space=pltpu.VMEM)
    hbm = pl.BlockSpec(memory_space=pltpu.HBM)
    return pl.pallas_call(
        store_kernel,
        out_shape=(
            jax.ShapeDtypeStruct(remapped.shape, F32),
            jax.ShapeDtypeStruct(accel.shape, F32),
        ),
        in_specs=[vmem, vmem],
        out_specs=(hbm, hbm),
        scratch_shapes=[pltpu.SemaphoreType.DMA((2,))],
        compiler_params=pltpu.CompilerParams(vmem_limit_bytes=4 << 20),
        name="store",
    )(remapped, accel)


def per_device(src_fields, owner_peer, src_local, jac):
    source_tab, project_tab = remap_tables()
    tables = [*two_parts(source_tab), *two_parts(project_tab), *two_parts(force_table())]
    vmem = pl.BlockSpec(memory_space=pltpu.VMEM)
    hbm = pl.BlockSpec(memory_space=pltpu.HBM)
    dma = pltpu.SemaphoreType.DMA
    made = pl.pallas_call(
        whole_kernel,
        out_shape=(
            jax.ShapeDtypeStruct((ELEMS, WIDTH), F32),
            jax.ShapeDtypeStruct((ELEMS, 3 * NB), F32),
        ),
        in_specs=[hbm] * 10,
        out_specs=(vmem, vmem),
        scratch_shapes=[
            pltpu.VMEM((ELEMS, WIDTH), F32),
            *[pltpu.VMEM((ELEMS, WA), F32) for _ in range(NY)],
            *[pltpu.VMEM((ELEMS, WB), F32) for _ in range(NY)],
            pltpu.VMEM(((NX - 1) * NY * CAP, 1, WA), F32),
            pltpu.VMEM(((NX - 1) * NY * CAP, 1, WB), F32),
            pltpu.VMEM((SLOTS, 1, WA), F32),
            pltpu.VMEM((SLOTS, 1, WB), F32),
            pltpu.VMEM((2, ELEMS, WA), F32),
            pltpu.VMEM((2, ELEMS, WB), F32),
            pltpu.VMEM((2, ELEMS, 128), F32),
            pltpu.VMEM((NX * NY, 128), jnp.int32),
            pltpu.VMEM((NX - 1, NY, 128), jnp.int32),
            pltpu.VMEM((1, OVL * ELEMS), jnp.int32),
            pltpu.SMEM((NX, NY, 128), jnp.int32),
            pltpu.SMEM((1, OVL * ELEMS), jnp.int32),
            pltpu.VMEM((OVL, 1, ELEMS), jnp.int32),
            pltpu.VMEM((OVL, ELEMS), jnp.int32),
            pltpu.VMEM((ELEMS, OVL * QP), F32),
            pltpu.VMEM((OVL, NB, QP), BF16),
            pltpu.VMEM((OVL, NB, QP), BF16),
            pltpu.VMEM((OVL, QP, NB), BF16),
            pltpu.VMEM((OVL, QP, NB), BF16),
            pltpu.VMEM((NB, 768), BF16),
            pltpu.VMEM((NB, 768), BF16),
            pltpu.VMEM((2, 8, 256), F32),
            pltpu.VMEM((2, 8, 256), F32),
            pltpu.VMEM((2, 2, 8, 256), F32),
            pltpu.VMEM((2, 8, 256), F32),
            pltpu.VMEM((2, 8, 256), F32),
            pltpu.VMEM((2, 2, 8, 256), F32),
            pltpu.VMEM((2, 2, 8, 256), F32),
            pltpu.VMEM((2, 2, 8, 256), F32),
            pltpu.VMEM((2, 2, 8, 256), F32),
            pltpu.VMEM((2, 2, 2, 8, 256), F32),
            dma((2, 2, 8)),
            dma((2, 2, 8)),
            dma((NX - 1,)),
            dma((NX - 1,)),
            dma((2, NX - 1, NY)),
            dma((2, NX - 1, NY)),
            dma((5,)),
            dma((10,)),
            dma((26,)),
            dma((26,)),
        ],
        compiler_params=pltpu.CompilerParams(
            collective_id=0, has_side_effects=True, vmem_limit_bytes=30 << 20
        ),
        name="whole",
    )(
        pltpu.with_memory_space_constraint(src_fields, pltpu.HBM),
        pltpu.with_memory_space_constraint(jnp.transpose(owner_peer, (1, 2, 0)), pltpu.HBM),
        pltpu.with_memory_space_constraint(jnp.transpose(src_local, (1, 0)), pltpu.HBM),
        pltpu.with_memory_space_constraint(jac, pltpu.HBM),
        *[pltpu.with_memory_space_constraint(jnp.asarray(t), pltpu.HBM) for t in tables],
    )
    return store(*made)


def solution(mesh):
    placed = (
        P(("gx", "gy", "gz"), None),
        P(("gx", "gy", "gz"), None, None),
        P(("gx", "gy", "gz"), None),
        P(("gx", "gy", "gz"), None),
    )
    return jax.shard_map(
        per_device,
        mesh=mesh,
        in_specs=placed,
        out_specs=(P(("gx", "gy", "gz"), None), P(("gx", "gy", "gz"), None)),
        check_vma=False,
    )
```

time: 50.4 us -> 40.5 us (0.80)
  Pallas kernels: 46.5 us -> 39.8 us
  local copies, waits for them, and re-layouts: 3.12 us -> 0 us
    pallas_call x1, Pallas kernels: 46.5 us -> 39 us  [per_device(): pl.pallas_call(whole_kernel, out_shape=(jax.ShapeDtypeStruct((ELEMS, WIDT...]
    unnamed x2 -> x0, local copies, waits for them, and re-layouts: 3.12 us -> none
    pallas_call x0 -> x1, Pallas kernels: none -> 0.71 us  [store(): pl.pallas_call(store_kernel, out_shape=(jax.ShapeDtypeStruct(remapped.sha...]
where the time goes in v1:
time: 40.5 us; the launch traced here: 40.4 us
  Pallas kernels  39.8 us (98%)
  between operations  0.64 us (2%)
    pallas_call x1, Pallas kernels, per_device(): pl.pallas_call(whole_kernel, out_shape=(jax.ShapeDtypeStruct((ELEMS, WIDT...  39 us

profile of v1, /device:TPU:1, one launch (start us, length us, event | category | flops | bytes accessed | tf_op | source)
XLA Modules:
  0.0 40.4 jit_solution(8403225034098694467)
XLA Ops:
  0.6 39.0 %whole.1 = (f32[32,1080]{1,0:T(8,128)S(1)}, f32[32,648]{1,0:T(8,128)S(1)}) custom-call(f32[32,1080]{1,0:T(8,128)} %src_hbm.1, s32[8,1,32]{2,1,0:T(1,128)} %bitcast.2, s32[8,32]{1,0:T(8,128)} %bitcast.3, f32[32,4096]{1,0:T(8,128)} %jac_hbm.1, bf16[8,216,512]{2,1,0:T(8,128)(2,1)} %constant.12.clone.sh_hbm, bf16[8,216,512]{2,1,0:T(8,128)(2,1)} %constant.13.clone.sl_hbm, ...), custom_call_target="tpu_custom_call" | custom-call | tf_op jit(solution)/shard_map/whole/pallas_call | solution.py:571
  39.7 0.7 %store.1 = (f32[32,1080]{1,0:T(8,128)}, f32[32,648]{1,0:T(8,128)}) custom-call(f32[32,1080]{1,0:T(8,128)S(1)} %get-tuple-element.4.remapped_ref, f32[32,648]{1,0:T(8,128)S(1)} %get-tuple-element.5.accel_ref), custom_call_target="tpu_custom_call" | custom-call | tf_op jit(solution)/shard_map/store/pallas_call | solution.py:551

commit v2 on v1

--- a/solution.py
+++ b/solution.py
@@ -208,7 +208,7 @@
 def whole_kernel(
     src_hbm, owner_hbm, local_hbm, jac_hbm, sh_hbm, sl_hbm, ph_hbm, pl_hbm, fh_hbm, fl_hbm,
     remapped_ref, accel_ref,
-    src_v, a0, a1, a2, a3, a4, a5, a6, a7, b0, b1, b2, b3, b4, b5, b6, b7, send_a, send_b, arr_a, arr_b, rows_a, rows_b, rows_c,
+    src_v, a0, a1, a2, a3, a4, a5, a6, a7, b0, b1, b2, b3, b4, b5, b6, b7, send_a, send_b, arr_a, arr_b, rows_a, rows_b,
     req_v, rreq_v, pos_v, req_s, pos_s,
     owner_v, local_v, jac_v, sh_v, sl_v, ph_v, pl_v, fh_v, fl_v,
     face_x, face_y, face_z, got_x, got_y, got_z, got_xy, got_xz, got_yz, got_xyz,
@@ -339,6 +339,8 @@
 
     go(0, 0, 0)
     go(0, 1, 0)
+    go(1, 0, 0)
+    go(1, 1, 0)
     asked = [
         pltpu.make_async_copy(rreq_v.at[i - 1], req_s.at[i], copy_sem.at[i]) for i in range(1, NX)
     ]
@@ -362,8 +364,6 @@
     for i in range(1, NX):
         ask(i).wait_recv()
         asked[i - 1].start()
-    go(1, 0, 0)
-    go(1, 1, 0)
     for one in asked:
         one.wait()
 
@@ -405,7 +405,7 @@
         if j < 4:
             answer(0, 8 - j)
         pass_on(1, j)
-        for d in ((0,), (1, 7), (2, 6), (3, 5, 4))[j - 1]:
+        for d in ((0, 1, 7), (2, 6), (3, 5), (4,))[j - 1]:
             answer(1, d)
 
     for one in loads:
@@ -413,18 +413,15 @@
 
     def remap(part, extra):
         fields = (2, 3)[part]
-        held = (rows_a, rows_b)[part]
         total = jnp.zeros(((fields + extra) * ELEMS, NB), F32)
         for k in range(OVL):
-            buf = held.at[k % 2]
+            buf = rows_b.at[k % 2] if part else rows_a.at[k]
             for r in range(ELEMS):
                 at = jnp.clip(pos_s[0, k * ELEMS + r], 0, SLOTS - 1)
                 buf[pl.ds(r, 1), :] = incoming[part][at]
-                if part == 1:
-                    rows_c[k % 2, pl.ds(r, 1), :] = arr_a[at, :, WA - 128 :]
             rows = buf[...]
             if part == 1:
-                rows = jnp.concatenate([rows_c[k % 2][:, 128 - TAIL :], rows[:, : 3 * NB - TAIL]], 1)
+                rows = jnp.concatenate([rows_a[k, :, 2 * NB :], rows[:, : 3 * NB - TAIL]], 1)
             lhs = jnp.concatenate([rows[:, f * NB : (f + 1) * NB] for f in range(fields)], 0)
             values = dot3(lhs, sh_v[k], sl_v[k])
             weight = jac_v[:, k * QP : (k + 1) * QP]
@@ -455,8 +452,10 @@
                 dst = got_xz.at[1 - sx, 1 - sz]
             elif not offset[2]:
                 dst = got_xy.at[1 - sx, 1 - sy]
+                src, dst = src.at[pl.ds(6 * sy, 2)], dst.at[pl.ds(6 * sy, 2)]
             else:
                 dst = got_xyz.at[1 - sx, 1 - sy, 1 - sz]
+                src, dst = src.at[pl.ds(6 * sy, 2)], dst.at[pl.ds(6 * sy, 2)]
         elif offset[1]:
             src = face_y.at[sy]
             dst = got_yz.at[1 - sy, 1 - sz] if offset[2] else got_y.at[1 - sy]
@@ -584,9 +583,8 @@
             pltpu.VMEM(((NX - 1) * NY * CAP, 1, WB), F32),
             pltpu.VMEM((SLOTS, 1, WA), F32),
             pltpu.VMEM((SLOTS, 1, WB), F32),
-            pltpu.VMEM((2, ELEMS, WA), F32),
+            pltpu.VMEM((OVL, ELEMS, WA), F32),
             pltpu.VMEM((2, ELEMS, WB), F32),
-            pltpu.VMEM((2, ELEMS, 128), F32),
             pltpu.VMEM((NX * NY, 128), jnp.int32),
             pltpu.VMEM((NX - 1, NY, 128), jnp.int32),
             pltpu.VMEM((1, OVL * ELEMS), jnp.int32),

time: 40.5 us -> 38.3 us (0.946)
  Pallas kernels: 39.8 us -> 37.5 us
    pallas_call x1, Pallas kernels: 39 us -> 36.8 us  [per_device(): pl.pallas_call(whole_kernel, out_shape=(jax.ShapeDtypeStruct((ELEMS, WIDT...]
where the time goes in v2:
time: 38.3 us; the launch traced here: 38.1 us
  Pallas kernels  37.5 us (98%)
  between operations  0.64 us (2%)
    pallas_call x1, Pallas kernels, per_device(): pl.pallas_call(whole_kernel, out_shape=(jax.ShapeDtypeStruct((ELEMS, WIDT...  36.8 us

profile of v2, /device:TPU:1, one launch (start us, length us, event | category | flops | bytes accessed | tf_op | source)
XLA Modules:
  0.0 38.1 jit_solution(10983465813868681211)
XLA Ops:
  0.6 36.8 %whole.1 = (f32[32,1080]{1,0:T(8,128)S(1)}, f32[32,648]{1,0:T(8,128)S(1)}) custom-call(f32[32,1080]{1,0:T(8,128)} %src_hbm.1, s32[8,1,32]{2,1,0:T(1,128)} %bitcast.2, s32[8,32]{1,0:T(8,128)} %bitcast.3, f32[32,4096]{1,0:T(8,128)} %jac_hbm.1, bf16[8,216,512]{2,1,0:T(8,128)(2,1)} %constant.12.clone.sh_hbm, bf16[8,216,512]{2,1,0:T(8,128)(2,1)} %constant.13.clone.sl_hbm, ...), custom_call_target="tpu_custom_call" | custom-call | tf_op jit(solution)/shard_map/whole/pallas_call | solution.py:570
  37.4 0.7 %store.1 = (f32[32,1080]{1,0:T(8,128)}, f32[32,648]{1,0:T(8,128)}) custom-call(f32[32,1080]{1,0:T(8,128)S(1)} %get-tuple-element.4.remapped_ref, f32[32,648]{1,0:T(8,128)S(1)} %get-tuple-element.5.accel_ref), custom_call_target="tpu_custom_call" | custom-call | tf_op jit(solution)/shard_map/store/pallas_call | solution.py:550

commit v3 on v2

--- a/solution.py
+++ b/solution.py
@@ -399,13 +399,14 @@
                 reply(part, i, d).wait_recv()
 
     answer(0, 0)
+    answer(1, 0)
     for j in range(1, 5):
         pass_on(0, j)
         answer(0, j)
         if j < 4:
             answer(0, 8 - j)
         pass_on(1, j)
-        for d in ((0, 1, 7), (2, 6), (3, 5), (4,))[j - 1]:
+        for d in ((1, 7), (2, 6), (3, 5), (4,))[j - 1]:
             answer(1, d)
 
     for one in loads:

time: 38.3 us -> 38.1 us (level)
  no operation moved by 1% of the time
where the time goes in v3:
time: 38.1 us; the launch traced here: 38 us
  Pallas kernels  37.4 us (98%)
  between operations  0.64 us (2%)
    pallas_call x1, Pallas kernels, per_device(): pl.pallas_call(whole_kernel, out_shape=(jax.ShapeDtypeStruct((ELEMS, WIDT...  36.7 us

profile of v3, /device:TPU:1, one launch (start us, length us, event | category | flops | bytes accessed | tf_op | source)
XLA Modules:
  0.0 38.0 jit_solution(15954344047862488889)
XLA Ops:
  0.6 36.7 %whole.1 = (f32[32,1080]{1,0:T(8,128)S(1)}, f32[32,648]{1,0:T(8,128)S(1)}) custom-call(f32[32,1080]{1,0:T(8,128)} %src_hbm.1, s32[8,1,32]{2,1,0:T(1,128)} %bitcast.2, s32[8,32]{1,0:T(8,128)} %bitcast.3, f32[32,4096]{1,0:T(8,128)} %jac_hbm.1, bf16[8,216,512]{2,1,0:T(8,128)(2,1)} %constant.12.clone.sh_hbm, bf16[8,216,512]{2,1,0:T(8,128)(2,1)} %constant.13.clone.sl_hbm, ...), custom_call_target="tpu_custom_call" | custom-call | tf_op jit(solution)/shard_map/whole/pallas_call | solution.py:571
  37.3 0.7 %store.1 = (f32[32,1080]{1,0:T(8,128)}, f32[32,648]{1,0:T(8,128)}) custom-call(f32[32,1080]{1,0:T(8,128)S(1)} %get-tuple-element.4.remapped_ref, f32[32,648]{1,0:T(8,128)S(1)} %get-tuple-element.5.accel_ref), custom_call_target="tpu_custom_call" | custom-call | tf_op jit(solution)/shard_map/store/pallas_call | solution.py:551
